TPU v7x, 512 devices: a whole 4x8x8 slice. The times are simulated.
512 devices in a mesh: blk: 64 (over y_lo, z, core), rep: 8 (over y_hi, x).
Axes of the slice: x: 4, y: 8 (y_hi: 2, y_lo: 4; y = y_hi * 4 + y_lo), z: 8, core: 2. Of those that a mesh axis runs over, the one named last changes fastest.
Arguments:
- hidden_in: bfloat16 [8, 8192, 1536], P('rep', 'blk'), may hold values from -12 to 12
- lengths: int32 [512], P('rep'), may hold values from 1 to 128, 32768 in all
- routes: int32 [8, 8192, 8], P('rep', 'blk'), may hold values from 0 to 31, all different within a row; in each aligned block of 128 rows (0 to 127, 128 to 255, ..., all dimensions but the last counted through in order) at most 36 rows name the same one
- route_weights: float32 [8, 8192, 8], P('rep', 'blk'), may hold values from 0.03 to 0.3
- norm_gain: float32 [1536], replicated, may hold values from 0.1 to 1.9
- master: float32 [3, 1536, 64, 256], P(None, 'blk', None, 'rep'), may hold values from -1 to 1
- unembed: bfloat16 [32768, 1536], P('blk'), may hold values from -0.5 to 0.5
- final_gain: float32 [1536], replicated, may hold values from 0.5 to 1.5
- target_ids: int32 [512], P('rep'), may hold values from 0 to 32767
Outputs:
- hidden_out: bfloat16 [8, 8192, 1536], P('rep', 'blk')
- server_blocks: bfloat16 [3, 1536, 16384], P(None, None, 'blk')
- request_stats: float32 [3, 512], P(None, 'rep')
Inputs may be any that keep to these rules, and one draw needn't show every extreme that they name: `routes`: in the 128 slots of one device no expert is named by more than 36 slots, and in some device one expert is named by exactly 36. The lengths of all 512 prompts sum to 32768 and the longest is exactly 128.
All inputs are finite; a program needn't handle non-finite values. No bound on the sum of `lengths` on one device may be relied on, other than what follows from the above.
Results may differ from a plain program's by a relative error of at most 0.0022.
Values may be sent and summed in bfloat16 or wider, within the bound.
A program may use at most 128 MiB of HBM per device.

v0:
```python
import jax
import jax.numpy as jnp
from jax import lax
from jax.sharding import PartitionSpec as P

FF = 512
EXPERTS = 32
LEN = 128
CAP = 36


def merged(x, axis, combine):
    everything = jax.tree.map(lambda part: lax.all_gather(part, axis), x)
    initial = jax.tree.map(lambda part: part[0], everything)

    def turn(k, so_far):
        return combine(so_far, jax.tree.map(lambda part: part[k], everything))

    return lax.fori_loop(1, lax.axis_size(axis), turn, initial)


def combine_stats(first, second):
    return (first[0] + second[0], jnp.maximum(first[1], second[1]))


def local(
    hidden_in, lengths, routes, route_weights, norm_gain, master, unembed, final_gain, target_ids
):
    rows_here = hidden_in.shape[1]
    width = hidden_in.shape[2]
    top_count = routes.shape[2]
    blk_count = lax.axis_size("blk")
    rep_count = lax.axis_size("rep")
    blk_index = lax.axis_index("blk")
    unit_count = master.shape[3] * rep_count
    split_ways = max(1, FF // unit_count)
    local_exp = max(1, unit_count // FF)
    group_width = min(unit_count, FF)
    capacity = CAP
    blocks = master.astype(jnp.bfloat16)
    arrived_blocks = lax.all_to_all(blocks, "blk", split_axis=2, concat_axis=1, tiled=True)
    server = lax.all_gather(arrived_blocks, "rep", axis=3, tiled=True)[:, :, 0, :]
    gate_w = server[0].reshape(width, local_exp, group_width)
    up_w = server[1].reshape(width, local_exp, group_width)
    down_w = server[2].reshape(width, local_exp, group_width)
    prompts_here = lengths.shape[0]
    slot_index = blk_index * rows_here + jnp.arange(rows_here, dtype=jnp.int32)
    prompt_of = slot_index // LEN
    position = slot_index % LEN
    prompt_match = prompt_of[:, None] == jnp.arange(prompts_here, dtype=jnp.int32)[None, :]
    row_len = jnp.sum(jnp.where(prompt_match, lengths[None, :], 0), axis=1)
    is_valid = position < row_len
    resid_f = hidden_in[0].astype(jnp.float32)
    normed = (
        resid_f * lax.rsqrt(jnp.mean(resid_f * resid_f, axis=-1, keepdims=True) + 1e-05) * norm_gain
    ).astype(jnp.bfloat16)
    expert_ids = routes[0].reshape(-1)
    pair_live = jnp.repeat(is_valid, top_count)
    pair_row = jnp.repeat(jnp.arange(rows_here, dtype=jnp.int32), top_count)
    expert_hits = (
        (expert_ids[:, None] == jnp.arange(EXPERTS, dtype=jnp.int32)[None, :]) & pair_live[:, None]
    ).astype(jnp.int32)
    slot_rank = jnp.sum((jnp.cumsum(expert_hits, axis=0) - 1) * expert_hits, axis=1)
    slot_id = jnp.where(pair_live, expert_ids * capacity + slot_rank, EXPERTS * capacity)
    source_row = jnp.zeros((EXPERTS * capacity + 1,), jnp.int32).at[slot_id].set(pair_row)[:-1]
    filled = jnp.zeros((EXPERTS * capacity + 1,), jnp.bfloat16).at[slot_id].set(1.0)[:-1]
    outgoing = (normed[source_row] * filled[:, None]).reshape(EXPERTS, capacity, width)
    sending = jnp.repeat(outgoing, split_ways, axis=0).reshape(
        blk_count, local_exp, capacity, width
    )
    arrived = lax.all_to_all(sending, "blk", split_axis=0, concat_axis=0, tiled=True)
    sources = arrived.shape[0]
    slot_count = arrived.shape[2]
    stride = sources
    while stride % 2 == 0 and stride * local_exp * slot_count > 1024:
        stride = stride // 2
    grouped = arrived.reshape(sources // stride, stride, local_exp, slot_count, width)

    def one_block(portion):
        gate_out = jnp.einsum("slnd,dlf->slnf", portion, gate_w, preferred_element_type=jnp.float32)
        up_out = jnp.einsum("slnd,dlf->slnf", portion, up_w, preferred_element_type=jnp.float32)
        hidden = (jax.nn.silu(gate_out) * up_out).astype(jnp.bfloat16)
        return jnp.einsum(
            "slnf,dlf->slnd", hidden, down_w, preferred_element_type=jnp.float32
        ).astype(jnp.bfloat16)

    returned = lax.all_to_all(
        lax.map(one_block, grouped).reshape(sources, local_exp, slot_count, width),
        "blk",
        split_axis=0,
        concat_axis=0,
        tiled=True,
    )
    summed_f = jnp.sum(
        returned.reshape(EXPERTS, split_ways, capacity, width).astype(jnp.float32), axis=1
    )
    expert_out = lax.optimization_barrier(summed_f.astype(jnp.bfloat16)).reshape(
        EXPERTS * capacity, width
    )
    gather_index = jnp.where(pair_live, expert_ids * capacity + slot_rank, 0)
    pair_weight = route_weights[0].reshape(-1) * pair_live.astype(jnp.float32)
    moe = jnp.sum(
        (expert_out[gather_index].astype(jnp.float32) * pair_weight[:, None]).reshape(
            rows_here, top_count, width
        ),
        axis=1,
    )
    out_rows = (resid_f + moe).astype(jnp.bfloat16)
    out_f = out_rows.astype(jnp.float32)
    row_squares = jnp.sum(out_f * out_f, axis=-1) * is_valid.astype(jnp.float32)
    square_local = jnp.sum(jnp.where(prompt_match, row_squares[:, None], 0.0), axis=0)
    is_last = is_valid & (position == row_len - 1)
    picker = (prompt_match & is_last[:, None]).astype(jnp.bfloat16)
    last_local = lax.dot_general(
        picker, out_rows, (((0,), (0,)), ((), ())), preferred_element_type=jnp.float32
    )
    last_rows, square_total = lax.psum((last_local, square_local), "blk")
    norms = jnp.sqrt(square_total / (lengths.astype(jnp.float32) * width) + 1e-06)
    final = (
        last_rows
        * lax.rsqrt(jnp.mean(last_rows * last_rows, axis=-1, keepdims=True) + 1e-05)
        * final_gain
    ).astype(jnp.bfloat16)
    logits = lax.dot_general(
        final, unembed, (((1,), (1,)), ((), ())), preferred_element_type=jnp.float32
    )
    vocab_base = blk_index * unembed.shape[0]
    target_hit = (
        target_ids[:, None] == vocab_base + jnp.arange(unembed.shape[0], dtype=jnp.int32)[None, :]
    )
    target_part = jnp.sum(jnp.where(target_hit, logits, 0.0), axis=1)
    top_part = jnp.max(logits, axis=1)
    target_logit, top_logit = merged((target_part, top_part), "blk", combine_stats)
    request_stats = jnp.stack([norms, top_logit, target_logit])
    return (out_rows[None], server, request_stats)


def solution(mesh):
    return jax.shard_map(
        local,
        mesh=mesh,
        in_specs=(
            P("rep", "blk", None),
            P("rep"),
            P("rep", "blk", None),
            P("rep", "blk", None),
            P(),
            P(None, "blk", None, "rep"),
            P("blk", None),
            P(),
            P("rep"),
        ),
        out_specs=(P("rep", "blk", None), P(None, None, "blk"), P(None, "rep")),
        check_vma=False,
    )
```

profile of v0, /device:TPU:1, one launch (start us, length us, event | category | flops | bytes accessed | tf_op | source)
XLA Modules:
  0.0 1415.6 jit_solution(6448488277973749420)
XLA Ops:
  14.2 15.4 %all-to-all-start.1 = ((bf16[64,2,1152]{2,1,0:T(2,128)(2,1)}), bf16[64,2,1152]{2,1,0:T(2,128)(2,1)S(1)}, u32[]{:S(2)}, u32[]{:S(2)}) async-start(bf16[64,2,1152]{2,1,0:T(2,128)(2,1)} %reshape.309), calls=%async_computation.1 | async-start | bytes 589824 | tf_op jit(solution)/shard_map/all_to_all | solution.py:41
  30.7 9.0 reduce-window.6
  40.6 4.3 scatter_custom_fusion
  45.3 5.4 gather_fusion
  50.7 5.6 gather.9
  56.3 7.6 scatter_custom_fusion.1
  64.0 4.3 broadcast_multiply_fusion
  68.3 5.9 broadcast_in_dim.95
  74.3 10.9 all-to-all-start
  97.4 103.4 %all-gather.4.cloned.1.call-done = bf16[3,1536,1,256]{1,3,2,0:T(8,128)(2,1)} async-done(((bf16[3,1536,1,32]{1,3,2,0:T(8,128)(2,1)}), bf16[3,1536,1,256]{1,3,2,0:T(8,128)(2,1)}) %all-gather.4.cloned.1.call-update) | async-done | bytes 2359312 | tf_op jit(solution)/shard_map/all_gather | solution.py:42
  207.2 102.1 %all-to-all-done = bf16[64,1,36,1536]{3,2,1,0:T(8,128)(2,1)} async-done(((bf16[64,1,36,1536]{3,2,1,0:T(8,128)(2,1)}), bf16[64,1,36,1536]{3,2,1,0:T(8,128)(2,1)}, u32[]{:S(2)}, u32[]{:S(2)}) %all-to-all-start) | async-done | bytes 7077920 | tf_op jit(solution)/shard_map/all_to_all | solution.py:71
  309.2 30.4 %while.27 = (s32[]{:T(128)}, bf16[4,16,1,36,1536]{4,3,1,2,0:T(8,128)(2,1)}, bf16[4,16,1,36,1536]{4,3,1,2,0:T(8,128)(2,1)}, bf16[1536,1,256]{2,0,1:T(8,128)(2,1)}...) while((s32[]{:T(128)}, bf16[4,16,1,36,1536]{4,3,1,2,0:T(8,128)(2,1)}, ...), condition=%wide.region_8.9_spmd, body=%wide.region_7.8_spmd.sunk | while | flops 1360723968 | bytes 9438797 | solution.py:88
  311.6 5.2 fusion.84
  319.2 5.2 fusion.84
  326.8 5.2 fusion.84
  334.4 5.2 fusion.84
  339.7 27.5 %all-to-all-start.2 = ((bf16[64,1,36,1536]{3,2,1,0:T(8,128)(2,1)}), bf16[64,1,36,1536]{3,2,1,0:T(8,128)(2,1)}, u32[]{:S(2)}, u32[]{:S(2)}) async-start(bf16[64,1,36,1536]{3,2,1,0:T(8,128)(2,1)} %bitcast.167), calls=%async_computation.2 | async-start | bytes 15728640 | tf_op jit(solution)/shard_map/all_to_all | solution.py:87
  373.8 200.1 %all-to-all-done.2 = bf16[64,1,36,1536]{3,2,1,0:T(8,128)(2,1)} async-done(((bf16[64,1,36,1536]{3,2,1,0:T(8,128)(2,1)}), bf16[64,1,36,1536]{3,2,1,0:T(8,128)(2,1)}, u32[]{:S(2)}, u32[]{:S(2)}) %all-to-all-start.2) | async-done | bytes 7077920 | tf_op jit(solution)/shard_map/all_to_all | solution.py:87
  573.9 7.9 bitcast_reduce_fusion
  581.8 5.7 reshape.250
  587.5 9.7 gather_fusion.1
  597.3 4.7 fusion.39
  604.1 534.8 %all-reduce.5.cloned.1.call-done = f32[64,1536]{1,0:T(8,128)} async-done(((f32[64,1536]{1,0:T(8,128)}), f32[64,1536]{1,0:T(8,128)}) %all-reduce.5.cloned.1.call-update) | async-done | bytes 393232 | tf_op jit(solution)/shard_map/psum | solution.py:117
  1142.4 263.0 %all-reduce.2 = (f32[4096]{0:T(1024)S(1)}, f32[4096]{0:T(1024)S(1)}, f32[64]{0:T(128)S(1)}) all-reduce(f32[4096]{0:T(1024)S(1)} %dynamic-update-slice, f32[4096]{0:T(1024)S(1)} %dynamic-update-slice.1, f32[64]{0:T(128)S(1)} %select_reduce_fusion.1), channel_id=2, replica_groups=mesh['blk'=64,'rep'=8] {'blk'}, use_global_device_ids=true, to_apply=%add | all-reduce | flops 8256 | bytes 66048
  (165 shorter events, 53.4 us)
Async XLA Ops:
  7.2 1132.9 %copy-start = (bf16[512,1536]{1,0:T(8,128)(2,1)S(1)}, bf16[512,1536]{1,0:T(8,128)(2,1)}, u32[]{:S(2)}) copy-start(bf16[512,1536]{1,0:T(8,128)(2,1)} %param.19) | copy-start | bytes 4718596
  7.2 22.5 %copy-start.9 = (s32[64]{0:T(128)S(1)}, s32[64]{0:T(128)}, u32[]{:S(2)}) copy-start(s32[64]{0:T(128)} %param.14) | copy-start | bytes 772
  7.2 22.7 %copy-start.2 = (s32[1,128,8]{1,2,0:T(8,128)S(1)}, s32[1,128,8]{1,2,0:T(8,128)}, u32[]{:S(2)}) copy-start(s32[1,128,8]{1,2,0:T(8,128)} %param.15) | copy-start | bytes 12292
  7.2 37.7 %copy-start.1 = (bf16[1,128,1536]{2,1,0:T(8,128)(2,1)S(1)}, bf16[1,128,1536]{2,1,0:T(8,128)(2,1)}, u32[]{:S(2)}) copy-start(bf16[1,128,1536]{2,1,0:T(8,128)(2,1)} %param.13) | copy-start | bytes 1179652
  7.2 37.9 %copy-start.3 = (f32[1536]{0:T(1024)S(1)}, f32[1536]{0:T(1024)}, u32[]{:S(2)}) copy-start(f32[1536]{0:T(1024)} %param.17) | copy-start | bytes 18436
  14.2 54.1 %all-to-all-start.1 = ((bf16[64,2,1152]{2,1,0:T(2,128)(2,1)}), bf16[64,2,1152]{2,1,0:T(2,128)(2,1)S(1)}, u32[]{:S(2)}, u32[]{:S(2)}) async-start(bf16[64,2,1152]{2,1,0:T(2,128)(2,1)} %reshape.309), calls=%async_computation.1 | async-start | bytes 589824 | tf_op jit(solution)/shard_map/all_to_all | solution.py:41
  29.7 0.7 copy-start.6
  74.3 235.0 %all-to-all-start = ((bf16[64,1,36,1536]{3,2,1,0:T(8,128)(2,1)}), bf16[64,1,36,1536]{3,2,1,0:T(8,128)(2,1)}, u32[]{:S(2)}, u32[]{:S(2)}) async-start(bf16[64,1,36,1536]{3,2,1,0:T(8,128)(2,1)} %bitcast.165), calls=%async_computation | async-start | bytes 15728640 | tf_op jit(solution)/shard_map/all_to_all | solution.py:71
  85.2 115.6 %all-gather.4.cloned.1.call-start = ((), (), s32[]{:S(2)}) async-start(), calls=%async_computation.3 | async-start | bytes 2654208 | tf_op jit(solution)/shard_map/all_gather | solution.py:42
  339.7 27.8 %copy-start.5 = (f32[1,128,8]{1,2,0:T(8,128)S(1)}, f32[1,128,8]{1,2,0:T(8,128)}, u32[]{:S(2)}) copy-start(f32[1,128,8]{1,2,0:T(8,128)} %param.16) | copy-start | bytes 12292
  339.7 234.2 %all-to-all-start.2 = ((bf16[64,1,36,1536]{3,2,1,0:T(8,128)(2,1)}), bf16[64,1,36,1536]{3,2,1,0:T(8,128)(2,1)}, u32[]{:S(2)}, u32[]{:S(2)}) async-start(bf16[64,1,36,1536]{3,2,1,0:T(8,128)(2,1)} %bitcast.167), calls=%async_computation.2 | async-start | bytes 15728640 | tf_op jit(solution)/shard_map/all_to_all | solution.py:87
  367.2 771.8 %all-reduce.5.cloned.1.call-start = ((), (), s32[]{:S(2)}) async-start(), calls=%async_computation.4 | async-start | bytes 786432 | tf_op jit(solution)/shard_map/psum | solution.py:117
  597.3 4.9 copy-start.7
  602.0 538.1 %copy-start.4 = (f32[1536]{0:T(1024)S(1)}, f32[1536]{0:T(1024)}, u32[]{:S(2)}) copy-start(f32[1536]{0:T(1024)} %param.20) | copy-start | bytes 18436
  602.0 538.1 %copy-start.8 = (s32[64]{0:T(128)S(1)}, s32[64]{0:T(128)}, u32[]{:S(2)}) copy-start(s32[64]{0:T(128)} %param.21) | copy-start | bytes 772
  602.0 806.2 %copy-start.10 = (s32[64]{0:T(128)S(1)}, s32[64]{0:T(128)}, u32[]{:S(2)}) copy-start(s32[64]{0:T(128)} %param.14) | copy-start | bytes 772
Sparse Core Ops, SparseCore 0:
  97.5 103.2 all-gather.3
  603.3 535.6 all-reduce.4
where the time goes:
time: 1420 us
  waiting for transfers between devices  940 us (66%)
  blocking collectives  263 us (19%)
  local copies, waits for them, and re-layouts  76.2 us (5%)
  starting transfers between devices  54.1 us (4%)
  matrix products  33.1 us (2%)
  other arithmetic  32.2 us (2%)
  between operations  15.1 us (1%)
    psum x1, waiting for transfers between devices, local(): last_rows, square_total = lax.psum((last_local, square_local), 'blk')  535 us
    unnamed x1, blocking collectives  263 us
    all_to_all x1, waiting for transfers between devices, local(): lax.all_to_all(lax.map(one_block, grouped).reshape(sources, local_exp, sl...  200 us
    all_gather x1, waiting for transfers between devices, local(): lax.all_gather(arrived_blocks, 'rep', axis=3, tiled=True)[:, :, 0, :]  103 us
    all_to_all x1, waiting for transfers between devices, local(): lax.all_to_all(sending, 'blk', split_axis=0, concat_axis=0, tiled=True)  102 us
  transfers between devices with their start and end apart: 5, of which 4 were waited for; matrix products, arithmetic and copies ran while one was open for 4% of the time, Pallas kernels for 0%

commit v1 on v0

v1 whole, which is shorter than its diff:
```python
import functools

import jax
import jax.numpy as jnp
from jax import lax
from jax.experimental import pallas as pl
from jax.experimental.pallas import tpu as pltpu
from jax.sharding import PartitionSpec as P

FF = 512
EXPERTS = 32
LEN = 128
CAP = 36
MESH = pl.DeviceIdType.MESH


def greet(count, me):
    barrier = pltpu.get_barrier_semaphore()

    def signal(i, carry):
        peer = lax.rem(me + i, count)
        pl.semaphore_signal(barrier, inc=1, device_id={"blk": peer}, device_id_type=MESH)
        return carry

    lax.fori_loop(1, count, signal, 0)
    pl.semaphore_wait(barrier, count - 1)


def exchange(count, me, make):
    def send(i, carry):
        make(lax.rem(me + i, count), me).start()
        return carry

    def finish(i, carry):
        make(lax.rem(me + i, count), lax.rem(me + i, count)).wait()
        return carry

    lax.fori_loop(1, count, send, 0)
    lax.fori_loop(1, count, finish, 0)


def tail_kernel(
    count, width, row_ref, unembed_ref, target_ref, length_ref, out_ref,
    rows, parts, send_a, recv_a, send_b, recv_b,
):
    me = lax.axis_index("blk")
    greet(count, me)
    rows[me] = row_ref[...]

    def row_copy(peer, slot):
        return pltpu.make_async_remote_copy(
            src_ref=row_ref, dst_ref=rows.at[slot], send_sem=send_a.at[peer],
            recv_sem=recv_a.at[slot], device_id={"blk": peer}, device_id_type=MESH,
        )

    exchange(count, me, row_copy)
    gathered = rows[...].reshape(count, width + 128)
    final = gathered[:, :width].astype(jnp.bfloat16)
    logits = lax.dot_general(
        unembed_ref[...], final, (((1,), (1,)), ((), ())), preferred_element_type=jnp.float32
    )
    vocab = lax.broadcasted_iota(jnp.int32, logits.shape, 0) + me * logits.shape[0]
    hit = vocab == target_ref[...]
    top = jnp.max(logits, axis=0, keepdims=True)
    target = jnp.sum(jnp.where(hit, logits, 0.0), axis=0, keepdims=True)
    parts[me] = jnp.concatenate([top, target], axis=0)

    def part_copy(peer, slot):
        return pltpu.make_async_remote_copy(
            src_ref=parts.at[me], dst_ref=parts.at[slot], send_sem=send_b.at[peer],
            recv_sem=recv_b.at[slot], device_id={"blk": peer}, device_id_type=MESH,
        )

    exchange(count, me, part_copy)
    squares = gathered[:, width : width + count]
    diagonal = lax.broadcasted_iota(jnp.int32, squares.shape, 0) == lax.broadcasted_iota(
        jnp.int32, squares.shape, 1
    )
    square = jnp.sum(jnp.where(diagonal, squares, 0.0), axis=0, keepdims=True)
    lengths = length_ref[...].astype(jnp.float32)
    out_ref[0:1, :] = jnp.sqrt(square / (lengths * width) + 1e-06)
    everything = parts[...]
    out_ref[1:2, :] = jnp.max(everything[:, 0, :], axis=0, keepdims=True)
    out_ref[2:3, :] = jnp.sum(everything[:, 1, :], axis=0, keepdims=True)


def tail(row, unembed, target_ids, lengths, count):
    width = unembed.shape[1]
    vmem = pl.BlockSpec(memory_space=pltpu.VMEM)
    return pl.pallas_call(
        functools.partial(tail_kernel, count, width),
        out_shape=jax.ShapeDtypeStruct((3, count), jnp.float32),
        in_specs=[vmem] * 4,
        out_specs=vmem,
        scratch_shapes=[
            pltpu.VMEM((count, 1, width + 128), jnp.float32),
            pltpu.VMEM((count, 2, count), jnp.float32),
            pltpu.SemaphoreType.DMA((count,)),
            pltpu.SemaphoreType.DMA((count,)),
            pltpu.SemaphoreType.DMA((count,)),
            pltpu.SemaphoreType.DMA((count,)),
        ],
        compiler_params=pltpu.CompilerParams(
            collective_id=1, has_side_effects=True, vmem_limit_bytes=32 << 20
        ),
    )(row, unembed, target_ids[None], lengths[None])


def local(
    hidden_in, lengths, routes, route_weights, norm_gain, master, unembed, final_gain, target_ids
):
    rows_here, width = hidden_in.shape[1:]
    blk_count = lax.axis_size("blk")
    blk_index = lax.axis_index("blk")
    blocks = master.astype(jnp.bfloat16)
    arrived_blocks = lax.all_to_all(blocks, "blk", split_axis=2, concat_axis=1, tiled=True)
    server = lax.all_gather(arrived_blocks, "rep", axis=3, tiled=True)[:, :, 0, :]
    partner = lax.ppermute(server, "blk", [(i, i ^ 1) for i in range(blk_count)])

    row_len = jnp.sum(
        jnp.where(jnp.arange(lengths.shape[0], dtype=jnp.int32) == blk_index, lengths, 0)
    )
    position = jnp.arange(rows_here, dtype=jnp.int32)
    is_valid = position < row_len
    resid_f = hidden_in[0].astype(jnp.float32)
    normed = (
        resid_f * lax.rsqrt(jnp.mean(resid_f * resid_f, axis=-1, keepdims=True) + 1e-05) * norm_gain
    ).astype(jnp.bfloat16)
    named = routes[0][:, :, None] == jnp.arange(EXPERTS, dtype=jnp.int32)
    named = named & is_valid[:, None, None]
    weight = jnp.sum(jnp.where(named, route_weights[0][:, :, None], 0.0), axis=1)
    hits = jnp.any(named, axis=1)
    before = (position[:, None] > position[None, :]).astype(jnp.bfloat16)
    rank = lax.dot_general(
        before, hits.astype(jnp.bfloat16), (((1,), (0,)), ((), ())),
        preferred_element_type=jnp.float32,
    ).astype(jnp.int32)
    place = hits[:, :, None] & (rank[:, :, None] == jnp.arange(CAP, dtype=jnp.int32))
    picker = place.reshape(rows_here, EXPERTS * CAP)
    sending = lax.dot_general(
        picker.astype(jnp.bfloat16), normed, (((0,), (0,)), ((), ())),
        preferred_element_type=jnp.float32,
    ).astype(jnp.bfloat16).reshape(EXPERTS, CAP, width)
    groups = [list(range(0, blk_count, 2)), list(range(1, blk_count, 2))]
    arrived = lax.all_to_all(
        sending, "blk", split_axis=0, concat_axis=0, tiled=True, axis_index_groups=groups
    )

    def half(rows, blocks):
        gate_out = jnp.dot(rows, blocks[0], preferred_element_type=jnp.float32)
        up_out = jnp.dot(rows, blocks[1], preferred_element_type=jnp.float32)
        hidden = (jax.nn.silu(gate_out) * up_out).astype(jnp.bfloat16)
        part = lax.dot_general(
            hidden, blocks[2], (((1,), (1,)), ((), ())), preferred_element_type=jnp.float32
        )
        return lax.reduce_precision(part, 8, 7)

    flat = arrived.reshape(EXPERTS * CAP, width)
    expert_out = (half(flat, server) + half(flat, partner)).astype(jnp.bfloat16)
    returned = lax.all_to_all(
        expert_out.reshape(EXPERTS, CAP, width), "blk", split_axis=0, concat_axis=0, tiled=True,
        axis_index_groups=groups,
    ).reshape(EXPERTS * CAP, width)
    spread = jnp.where(place, weight[:, :, None], 0.0).reshape(rows_here, EXPERTS * CAP)
    moe = 0.0
    left = spread
    for _ in range(3):
        piece = lax.reduce_precision(left, 8, 7)
        left = left - piece
        moe = moe + jnp.dot(
            piece.astype(jnp.bfloat16), returned, preferred_element_type=jnp.float32
        )
    out_rows = (resid_f + moe).astype(jnp.bfloat16)
    out_f = out_rows.astype(jnp.float32)
    square = jnp.sum(jnp.where(is_valid[:, None], out_f * out_f, 0.0))
    last = jnp.sum(jnp.where((position == row_len - 1)[:, None], out_f, 0.0), axis=0)
    final = last * lax.rsqrt(jnp.mean(last * last) + 1e-05) * final_gain
    final = lax.reduce_precision(final, 8, 7)
    row = jnp.concatenate([final, jnp.full((128,), square)])[None]
    request_stats = tail(row, unembed, target_ids, lengths, blk_count)
    return (out_rows[None], server, request_stats)


def solution(mesh):
    return jax.shard_map(
        local,
        mesh=mesh,
        in_specs=(
            P("rep", "blk", None),
            P("rep"),
            P("rep", "blk", None),
            P("rep", "blk", None),
            P(),
            P(None, "blk", None, "rep"),
            P("blk", None),
            P(),
            P("rep"),
        ),
        out_specs=(P("rep", "blk", None), P(None, None, "blk"), P(None, "rep")),
        check_vma=False,
    )
```

time: 1420 us -> 414 us (0.29)
  the two profiles are of different devices: /device:TPU:1 before, /device:TPU:57 now
where the time goes in v1:
time: 414 us; the launch traced here: 413 us
  waiting for transfers between devices  218 us (53%)
  Pallas kernels  58.6 us (14%)
  starting transfers between devices  51.3 us (12%)
  matrix products  37.1 us (9%)
  local copies, waits for them, and re-layouts  28.7 us (7%)
  between operations  15.7 us (4%)
    all_gather x1, waiting for transfers between devices, local(): lax.all_gather(arrived_blocks, 'rep', axis=3, tiled=True)[:, :, 0, :]  104 us
    all_to_all x1, waiting for transfers between devices, local(): lax.all_to_all(expert_out.reshape(EXPERTS, CAP, width), 'blk', split_axis...  95.1 us
    pallas_call x1, Pallas kernels, tail(): pl.pallas_call(functools.partial(tail_kernel, count, width), out_shape=ja...  58.6 us
    all_to_all x1, starting transfers between devices, local(): lax.all_to_all(expert_out.reshape(EXPERTS, CAP, width), 'blk', split_axis...  28.2 us
    dot_general x2, matrix products, half(): lax.dot_general(hidden, blocks[2], (((1,), (1,)), ((), ())), preferred_el...  17.8 us
    all_to_all x1, starting transfers between devices, local(): lax.all_to_all(blocks, 'blk', split_axis=2, concat_axis=1, tiled=True)  14.8 us
    all_to_all x1, waiting for transfers between devices, local(): lax.all_to_all(sending, 'blk', split_axis=0, concat_axis=0, tiled=True, a...  14.2 us
    dot_general x3, matrix products, local(): jnp.dot(piece.astype(jnp.bfloat16), returned, preferred_element_type=jnp....  10.4 us
  transfers between devices with their start and end apart: 5, of which 4 were waited for; matrix products, arithmetic and copies ran while one was open for 7% of the time, Pallas kernels for 0%

profile of v1, /device:TPU:57, one launch (start us, length us, event | category | flops | bytes accessed | tf_op | source)
XLA Modules:
  0.0 413.1 jit_solution(12603940805554661310)
XLA Ops:
  12.2 14.8 %all-to-all-start.1 = ((bf16[64,2,1152]{2,1,0:T(2,128)(2,1)}), bf16[64,2,1152]{2,1,0:T(2,128)(2,1)}, u32[]{:S(2)}, u32[]{:S(2)}) async-start(bf16[64,2,1152]{2,1,0:T(2,128)(2,1)} %reshape.131), calls=%async_computation.1 | async-start | bytes 589824 | tf_op jit(solution)/shard_map/all_to_all | solution.py:116
  29.6 2.2 convolution_convert_fusion
  31.8 2.6 reshape.124
  34.3 4.7 %all-to-all-done.1 = bf16[64,2,1152]{2,1,0:T(2,128)(2,1)} async-done(((bf16[64,2,1152]{2,1,0:T(2,128)(2,1)}), bf16[64,2,1152]{2,1,0:T(2,128)(2,1)}, u32[]{:S(2)}, u32[]{:S(2)}) %all-to-all-start.1) | async-done | bytes 294944 | tf_op jit(solution)/shard_map/all_to_all | solution.py:116
  39.0 5.1 %all-to-all-start = ((bf16[32,36,1536]{2,1,0:T(8,128)(2,1)}), bf16[32,36,1536]{2,1,0:T(8,128)(2,1)}, u32[]{:S(2)}, u32[]{:S(2)}) async-start(bf16[32,36,1536]{2,1,0:T(8,128)(2,1)} %reshape.124), calls=%async_computation | async-start | bytes 7864320 | tf_op jit(solution)/shard_map/all_to_all | solution.py:145
  44.1 2.2 reshape.132
  46.5 2.5 copy.33
  49.1 3.7 all_to_all.23
  52.8 104.2 %all-gather.2.cloned.1.call-done = bf16[3,1536,1,256]{1,3,2,0:T(8,128)(2,1)} async-done(((bf16[3,1536,1,32]{1,3,2,0:T(8,128)(2,1)}), bf16[3,1536,1,256]{1,3,2,0:T(8,128)(2,1)}) %all-gather.2.cloned.1.call-update) | async-done | bytes 2359312 | tf_op jit(solution)/shard_map/all_gather | solution.py:117
  157.0 3.1 collective-permute-start
  160.1 14.2 %all-to-all-done = bf16[32,36,1536]{2,1,0:T(8,128)(2,1)} async-done(((bf16[32,36,1536]{2,1,0:T(8,128)(2,1)}), bf16[32,36,1536]{2,1,0:T(8,128)(2,1)}, u32[]{:S(2)}, u32[]{:S(2)}) %all-to-all-start) | async-done | bytes 3538976 | tf_op jit(solution)/shard_map/all_to_all | solution.py:145
  174.3 3.9 reshape.125
  178.2 3.3 fusion.21
  181.5 8.3 %convolution_reduce-precision_fusion.1 = f32[1152,1536]{1,0:T(8,128)} fusion(bf16[1152,1536]{1,0:T(8,128)(2,1)S(1)} %reshape.125, f32[1152,256]{1,0:T(8,128)} %fusion.21, bf16[3,1536,1,256]{1,3,2,0:T(8,128)(2,1)} %all-gather.2.cloned.1.call-done), kind=kOutput, calls=%fused_computation.2 | convolution fusion | flops 1815478272 | bytes 13369344 | tf_op jit(solution)/shard_map/dot_general | solution.py:153
  189.8 3.3 fusion.20
  193.1 9.5 %fusion.1 = bf16[1152,1536]{1,0:T(8,128)(2,1)} fusion(f32[1152,1536]{1,0:T(8,128)} %convolution_reduce-precision_fusion.1, bf16[3,1536,256]{1,2,0:T(8,128)(2,1)} %collective-permute-done, f32[1152,256]{1,0:T(8,128)} %fusion.20, bf16[1152,1536]{1,0:T(8,128)(2,1)S(1)} %reshape.125), kind=kOutput, calls=%fused_computation.3 | convolution fusion | flops 1819017216 | bytes 16908288 | tf_op jit(solution)/shard_map/dot_general | solution.py:153
  202.6 5.7 %reshape.126 = bf16[32,36,1536]{2,1,0:T(8,128)(2,1)} reshape(bf16[1152,1536]{1,0:T(8,128)(2,1)} %fusion.1) | data formatting | bytes 7077888 | tf_op jit(solution)/shard_map/reshape | solution.py:161
  208.2 28.2 %all-to-all-start.2 = ((bf16[32,36,1536]{2,1,0:T(8,128)(2,1)}), bf16[32,36,1536]{2,1,0:T(8,128)(2,1)}, u32[]{:S(2)}, u32[]{:S(2)}) async-start(bf16[32,36,1536]{2,1,0:T(8,128)(2,1)} %reshape.126), calls=%async_computation.2 | async-start | bytes 7864320 | tf_op jit(solution)/shard_map/all_to_all | solution.py:160
  237.2 2.4 copy.35
  239.6 95.1 %all-to-all-done.2 = bf16[32,36,1536]{2,1,0:T(8,128)(2,1)} async-done(((bf16[32,36,1536]{2,1,0:T(8,128)(2,1)}), bf16[32,36,1536]{2,1,0:T(8,128)(2,1)}, u32[]{:S(2)}, u32[]{:S(2)}) %all-to-all-start.2) | async-done | bytes 3538976 | tf_op jit(solution)/shard_map/all_to_all | solution.py:160
  334.7 2.9 convolution_bitcast_fusion.1
  337.6 3.0 convolution_bitcast_fusion
  340.7 4.5 %fusion.15 = (f32[]{:T(128)}, f32[1536]{0:T(1024)S(1)}, bf16[128,1536]{1,0:T(8,128)(2,1)}) fusion(pred[128]{0:T(512)(128)(4,1)S(1)} %iota_compare_fusion.5, pred[128]{0:T(512)(128)(4,1)S(1)} %iota_compare_fusion.4, f32[128,1536]{1,0:T(8,128)S(1)} %convolution_bitcast_fusion, f32[128,1536]{1,0:T(8,128)S(1)} %convolution_bitcast_fusion.1, ...), kind=kOutput, calls=%fused_computation.32 | convolution fusion | flops 455883264 | bytes 5941508 | tf_op jit(solution)/shard_map/dot_general | solution.py:170
  347.2 58.6 %shard_map.112 = f32[3,64]{1,0:T(4,128)S(1)} custom-call(f32[1,1664]{1,0:T(1,128)S(1)} %broadcast_in_dim.83.row_ref, bf16[512,1536]{1,0:T(8,128)(2,1)S(1)} %copy-done, s32[1,64]{1,0:T(1,128)S(1)} %bitcast.78, s32[1,64]{1,0:T(1,128)S(1)} %bitcast.77), custom_call_target="tpu_custom_call" | custom-call | tf_op jit(solution)/shard_map/pallas_call | solution.py:90
  (44 shorter events, 9.7 us)
Async XLA Ops:
  8.5 18.5 %copy-start.1 = (s32[64]{0:T(128)S(1)}, s32[64]{0:T(128)}, u32[]{:S(2)}) copy-start(s32[64]{0:T(128)} %param.10) | copy-start | bytes 772
  8.6 19.7 %copy-start.8 = (s32[1,128,8]{1,2,0:T(8,128)S(1)}, s32[1,128,8]{1,2,0:T(8,128)}, u32[]{:S(2)}) copy-start(s32[1,128,8]{1,2,0:T(8,128)} %param.11) | copy-start | bytes 12292
  8.6 20.1 %copy-start.3 = (bf16[1,128,1536]{2,1,0:T(8,128)(2,1)S(1)}, bf16[1,128,1536]{2,1,0:T(8,128)(2,1)}, u32[]{:S(2)}) copy-start(bf16[1,128,1536]{2,1,0:T(8,128)(2,1)} %param.9) | copy-start | bytes 1179652
  12.2 26.8 %all-to-all-start.1 = ((bf16[64,2,1152]{2,1,0:T(2,128)(2,1)}), bf16[64,2,1152]{2,1,0:T(2,128)(2,1)}, u32[]{:S(2)}, u32[]{:S(2)}) async-start(bf16[64,2,1152]{2,1,0:T(2,128)(2,1)} %reshape.131), calls=%async_computation.1 | async-start | bytes 589824 | tf_op jit(solution)/shard_map/all_to_all | solution.py:116
  28.5 1.1 copy-start.6
  39.0 135.3 %all-to-all-start = ((bf16[32,36,1536]{2,1,0:T(8,128)(2,1)}), bf16[32,36,1536]{2,1,0:T(8,128)(2,1)}, u32[]{:S(2)}, u32[]{:S(2)}) async-start(bf16[32,36,1536]{2,1,0:T(8,128)(2,1)} %reshape.124), calls=%async_computation | async-start | bytes 7864320 | tf_op jit(solution)/shard_map/all_to_all | solution.py:145
  44.1 112.9 %all-gather.2.cloned.1.call-start = ((), (), s32[]{:S(2)}) async-start(), calls=%async_computation.3 | async-start | bytes 2654208 | tf_op jit(solution)/shard_map/all_gather | solution.py:117
  157.0 32.9 %collective-permute-start = (bf16[3,1536,256]{1,2,0:T(8,128)(2,1)}, bf16[3,1536,256]{1,2,0:T(8,128)(2,1)}, u32[]{:S(2)}, u32[]{:S(2)}) collective-permute-start(bf16[3,1536,256]{1,2,0:T(8,128)(2,1)} %bitcast.80), channel_id=1, source_target_pairs={{0,8},{8,0},{16,24},{24,16},{32,40},{40,32},{48,56},{56,48},{64,72... | collective-permute-start | bytes 7077896 | tf_op jit(solution)/shard_map/ppermute | solution.py:118
  208.2 28.9 %copy-start.10 = (f32[1,128,8]{1,2,0:T(8,128)S(1)}, f32[1,128,8]{1,2,0:T(8,128)}, u32[]{:S(2)}) copy-start(f32[1,128,8]{1,2,0:T(8,128)} %param.12) | copy-start | bytes 12292
  208.2 28.9 %copy-start.5 = (bf16[3,1536,1,256]{1,3,2,0:T(8,128)(2,1)S(1)}, bf16[3,1536,1,256]{1,3,2,0:T(8,128)(2,1)}, u32[]{:S(2)}) copy-start(bf16[3,1536,1,256]{1,3,2,0:T(8,128)(2,1)} %all-gather.2.cloned.1.call-done) | copy-start | bytes 7077892
  208.2 126.5 %all-to-all-start.2 = ((bf16[32,36,1536]{2,1,0:T(8,128)(2,1)}), bf16[32,36,1536]{2,1,0:T(8,128)(2,1)}, u32[]{:S(2)}, u32[]{:S(2)}) async-start(bf16[32,36,1536]{2,1,0:T(8,128)(2,1)} %reshape.126), calls=%async_computation.2 | async-start | bytes 7864320 | tf_op jit(solution)/shard_map/all_to_all | solution.py:160
  237.2 97.5 %copy-start.7 = (s32[128,32]{0,1:T(8,128)S(1)}, s32[128,32]{0,1:T(8,128)}, u32[]{:S(2)}) copy-start(s32[128,32]{0,1:T(8,128)} %copy-done.6) | copy-start | bytes 49156
  337.6 3.0 copy-start.4
  340.6 5.8 %copy-start.9 = (f32[1536]{0:T(1024)S(1)}, f32[1536]{0:T(1024)}, u32[]{:S(2)}) copy-start(f32[1536]{0:T(1024)} %param.16) | copy-start | bytes 18436
  340.6 6.5 %copy-start = (bf16[512,1536]{1,0:T(8,128)(2,1)S(1)}, bf16[512,1536]{1,0:T(8,128)(2,1)}, u32[]{:S(2)}) copy-start(bf16[512,1536]{1,0:T(8,128)(2,1)} %unembed_ref.1) | copy-start | bytes 4718596
  340.7 6.5 %copy-start.2 = (s32[64]{0:T(128)S(1)}, s32[64]{0:T(128)}, u32[]{:S(2)}) copy-start(s32[64]{0:T(128)} %param.17) | copy-start | bytes 772
Sparse Core Ops, SparseCore 0:
  52.9 104.0 all-gather.1
